TPU v7x, 32 devices: a whole 2x2x4 slice. The times are simulated.
32 devices in a mesh: blk: 8 (over y, x, core), fsdp: 4 (over z).
Axes of the slice: x: 2, y: 2, z: 4, core: 2. Of those that a mesh axis runs over, the one named last changes fastest.
Arguments:
- hidden: bfloat16 [8, 512, 5120], P('blk', 'fsdp'), may hold values from -6 to 6
- grad_query: bfloat16 [8, 512, 5120], P('blk', 'fsdp'), may hold values from -6 to 6
- grad_value: bfloat16 [8, 512, 5120], P('blk', 'fsdp'), may hold values from -6 to 6
- adapters: bfloat16 [8, 192, 5120], P('blk', 'fsdp'), may hold values from -4 to 4
- first_moment: bfloat16 [8, 192, 5120], P('blk', 'fsdp'), may hold values from -0.009765625 to 0.009765625
- second_moment: bfloat16 [8, 192, 5120], P('blk', 'fsdp'), may hold values from 8.090865e-09 to 8.1025064e-08
- mixing: int32 [8, 3], P('blk'), may hold values from 1 to 2, as said below
Outputs:
- mixed: bfloat16 [8, 192, 5120], P('blk', 'fsdp')
Inputs may be any that keep to these rules, and one draw needn't show every extreme that they name: `mixing`: each row holds two numerators equal to 1 and one equal to 2.
All inputs are finite; a program needn't handle non-finite values.
Results may differ from a plain program's by a relative error of at most 0.0051.
Values may be sent and summed in bfloat16 or wider, within the bound.
A program may use at most 64 MiB of HBM per device.

v0:
```python
import math

import jax
import jax.numpy as jnp
from jax import lax
from jax.sharding import PartitionSpec as P

beta_one = 0.9
beta_two = 0.999
learn_rate = 0.2
decay_rate = 0.5
epsilon = 1e-08


def shifted(array, axis, by):
    length = lax.axis_size(axis)
    return lax.ppermute(array, axis, [(i, (i + by) % length) for i in range(length)])


def contract_tokens(left, right, scale):
    return (
        lax.dot_general(left, right, (((0,), (0,)), ((), ())), preferred_element_type=jnp.float32)
        * scale
    )


def shards(hidden, grad_query, grad_value, adapters, first_moment, second_moment, mixing):
    tokens = hidden[0]
    width = tokens.shape[1]
    full_rows = lax.all_gather(adapters, "fsdp", axis=1, tiled=True)[0]
    rank = full_rows.shape[0] // 4
    inv_width = 1.0 / math.sqrt(width)
    inv_rank = 1.0 / math.sqrt(rank)
    factors = []
    for index, cot in ((0, grad_query[0]), (1, grad_value[0])):
        down = full_rows[2 * index * rank : (2 * index + 1) * rank]
        up_rows = full_rows[(2 * index + 1) * rank : (2 * index + 2) * rank]
        lowrank = (jnp.dot(tokens, down.T, preferred_element_type=jnp.float32) * inv_width).astype(
            jnp.bfloat16
        )
        back = (jnp.dot(cot, up_rows.T, preferred_element_type=jnp.float32) * inv_rank).astype(
            jnp.bfloat16
        )
        factors.append((back, tokens, inv_width))
        factors.append((lowrank, cot, inv_rank))
    shard_rows = adapters.shape[1]
    group_tokens = tokens.shape[0] * lax.axis_size("fsdp")
    weights = mixing[0].astype(jnp.float32)
    term = jnp.concatenate(
        [contract_tokens(left, right, scale) for left, right, scale in factors], axis=0
    )

    def owned_rows(start, count, term=term):
        return term

    gradient = (
        lax.psum_scatter(
            owned_rows(jnp.int32(0), lax.axis_size("fsdp") * shard_rows).astype(jnp.bfloat16),
            "fsdp",
            scatter_dimension=0,
            tiled=True,
        ).astype(jnp.float32)
        / group_tokens
    )
    params = adapters[0].astype(jnp.float32)
    first = first_moment[0].astype(jnp.float32)
    second = second_moment[0].astype(jnp.float32)
    new_first = beta_one * first + (1.0 - beta_one) * gradient
    new_second = beta_two * second + (1.0 - beta_two) * gradient * gradient
    first_hat = new_first / (1.0 - beta_one**2)
    second_hat = new_second / (1.0 - beta_two**2)
    step = first_hat / (jnp.sqrt(second_hat) + epsilon) + decay_rate * params
    updated = (params - learn_rate * step).astype(jnp.bfloat16)
    lower = shifted(updated, "blk", 1)
    upper = shifted(updated, "blk", -1)
    total = weights[0] * lower.astype(jnp.float32) + weights[1] * updated.astype(jnp.float32)
    total = total + weights[2] * upper.astype(jnp.float32)
    results = (total / 4.0).astype(jnp.bfloat16)
    return results[None]


def solution(mesh):
    in_specs = (
        P("blk", "fsdp", None),
        P("blk", "fsdp", None),
        P("blk", "fsdp", None),
        P("blk", "fsdp", None),
        P("blk", "fsdp", None),
        P("blk", "fsdp", None),
        P("blk", None),
    )
    out_specs = P("blk", "fsdp", None)
    return jax.shard_map(shards, mesh=mesh, in_specs=in_specs, out_specs=out_specs, check_vma=False)
```

profile of v0, /device:TPU:11, one launch (start us, length us, event | category | flops | bytes accessed | tf_op | source)
XLA Modules:
  0.0 134.1 jit_solution(4167797149082029256)
XLA Ops:
  6.5 0.0 copy-start
  6.5 0.0 all-gather.2.cloned.1.call-start
  6.5 0.7 all-gather.2.cloned.1.call-update
  7.3 0.0 copy-start.1
  7.3 0.0 reduce-scatter.2.cloned.1.call-start
  7.3 44.8 %all-gather.2.cloned.1.call-done = bf16[1,192,5120]{2,1,0:T(8,128)(2,1)} async-done(((bf16[1,48,5120]{2,1,0:T(8,128)(2,1)}), bf16[1,192,5120]{2,1,0:T(8,128)(2,1)}) %all-gather.2.cloned.1.call-update) | async-done | bytes 1966096 | tf_op jit(solution)/shard_map/all_gather | solution.py:30
  52.1 0.0 copy-done
  52.1 2.5 %fusion = bf16[48,5120]{1,0:T(8,128)(2,1)S(1)} fusion(bf16[1,128,5120]{2,1,0:T(8,128)(2,1)S(1)} %copy-done, bf16[1,128,5120]{2,1,0:T(8,128)(2,1)} %param.8, bf16[1,192,5120]{2,1,0:T(8,128)(2,1)} %all-gather.2.cloned.1.call-done), kind=kOutput, calls=%fused_computation.4 | convolution fusion | flops 126332928 | bytes 3604480 | tf_op jit(solution)/shard_map/dot_general | solution.py:22
  54.7 0.0 copy-done.1
  54.7 2.9 %fusion.1 = bf16[48,5120]{1,0:T(8,128)(2,1)} fusion(bf16[1,128,5120]{2,1,0:T(8,128)(2,1)S(1)} %copy-done.1, bf16[1,128,5120]{2,1,0:T(8,128)(2,1)S(1)} %copy-done, bf16[1,192,5120]{2,1,0:T(8,128)(2,1)} %all-gather.2.cloned.1.call-done), kind=kOutput, calls=%fused_computation.5 | convolution fusion | flops 126332928 | bytes 3604480 | tf_op jit(solution)/shard_map/dot_general | solution.py:22
  57.6 0.0 copy-start.2
  57.6 3.4 %fusion.2 = bf16[48,5120]{1,0:T(8,128)(2,1)} fusion(bf16[1,128,5120]{2,1,0:T(8,128)(2,1)S(1)} %copy-done, bf16[1,128,5120]{2,1,0:T(8,128)(2,1)} %param.9, bf16[1,192,5120]{2,1,0:T(8,128)(2,1)} %all-gather.2.cloned.1.call-done), kind=kOutput, calls=%fused_computation.6 | convolution fusion | flops 126332928 | bytes 3604480 | tf_op jit(solution)/shard_map/dot_general | solution.py:22
  61.1 0.0 copy-done.2
  61.1 2.9 %fusion.3 = bf16[48,5120]{1,0:T(8,128)(2,1)} fusion(bf16[1,128,5120]{2,1,0:T(8,128)(2,1)S(1)} %copy-done.2, bf16[1,128,5120]{2,1,0:T(8,128)(2,1)S(1)} %copy-done, bf16[1,192,5120]{2,1,0:T(8,128)(2,1)} %all-gather.2.cloned.1.call-done), kind=kOutput, calls=%fused_computation.7 | convolution fusion | flops 126332928 | bytes 3604480 | tf_op jit(solution)/shard_map/dot_general | solution.py:22
  64.0 2.8 %pad_maximum_fusion = bf16[192,5120]{1,0:T(8,128)(2,1)} fusion(bf16[48,5120]{1,0:T(8,128)(2,1)} %fusion.3, bf16[48,5120]{1,0:T(8,128)(2,1)} %fusion.2, bf16[48,5120]{1,0:T(8,128)(2,1)} %fusion.1, bf16[48,5120]{1,0:T(8,128)(2,1)S(1)} %fusion), kind=kLoop, calls=%fused_computation.8 | loop fusion | flops 7864320 | bytes 3932160 | tf_op jit(solution)/shard_map/concatenate | solution.py:49
  66.8 0.0 copy-start.3
  66.8 0.0 copy-start.4
  66.8 0.0 copy-start.5
  66.8 0.0 reduce-scatter.2.cloned.1.call-update
  66.8 0.0 copy-start.6
  66.8 41.1 %reduce-scatter.2.cloned.1.call-done = bf16[48,5120]{1,0:T(8,128)(2,1)} async-done(((bf16[192,5120]{1,0:T(8,128)(2,1)}), bf16[48,5120]{1,0:T(8,128)(2,1)}) %reduce-scatter.2.cloned.1.call-update) | async-done | bytes 491536 | tf_op jit(solution)/shard_map/reduce_scatter | solution.py:57
  107.9 0.0 copy-done.3
  107.9 0.0 copy-done.4
  107.9 0.0 copy-done.5
  107.9 1.9 %fusion.50 = bf16[48,5120]{1,0:T(8,128)(2,1)S(1)} fusion(bf16[48,5120]{1,0:T(8,128)(2,1)} %reduce-scatter.2.cloned.1.call-done, bf16[1,48,5120]{2,1,0:T(8,128)(2,1)S(1)} %copy-done.4, bf16[1,48,5120]{2,1,0:T(8,128)(2,1)S(1)} %copy-done.5, bf16[1,48,5120]{2,1,0:T(8,128)(2,1)S(1)} %copy-done.3), kind=kLoop, calls=%fused_computation.36 | loop fusion | flops 5160960 | bytes 2457600 | tf_op jit(solution)/shard_map/convert_element_type | solution.py:73
  109.9 1.8 %collective-permute-start = (bf16[48,5120]{1,0:T(8,128)(2,1)S(1)}, bf16[48,5120]{1,0:T(8,128)(2,1)S(1)}, u32[]{:S(2)}, u32[]{:S(2)}) collective-permute-start(bf16[48,5120]{1,0:T(8,128)(2,1)S(1)} %fusion.50), channel_id=1, source_target_pairs={{0,4},{4,8},{8,12},{12,16},{16,20},{20,24},{24,28},{28,0},{1,5},{5... | collective-permute-start | bytes 1474568 | tf_op jit(solution)/shard_map/ppermute | solution.py:17
  111.7 0.0 collective-permute-start.1
  111.7 0.0 copy-done.6
  111.7 0.6 fusion.68
  112.4 9.5 %collective-permute-done = bf16[48,5120]{1,0:T(8,128)(2,1)S(1)} collective-permute-done((bf16[48,5120]{1,0:T(8,128)(2,1)S(1)}, bf16[48,5120]{1,0:T(8,128)(2,1)S(1)}, u32[]{:S(2)}, u32[]{:S(2)}) %collective-permute-start) | collective-permute-done | bytes 491552 | tf_op jit(solution)/shard_map/ppermute | solution.py:17
  121.9 2.5 %collective-permute-done.1 = bf16[48,5120]{1,0:T(8,128)(2,1)S(1)} collective-permute-done((bf16[48,5120]{1,0:T(8,128)(2,1)S(1)}, bf16[48,5120]{1,0:T(8,128)(2,1)S(1)}, u32[]{:S(2)}, u32[]{:S(2)}) %collective-permute-start.1) | collective-permute-done | bytes 491552 | tf_op jit(solution)/shard_map/ppermute | solution.py:17
  124.4 2.9 %fusion.59 = bf16[1,48,5120]{2,1,0:T(8,128)(2,1)} fusion(bf16[48,5120]{1,0:T(8,128)(2,1)S(1)} %collective-permute-done.1, bf16[48,5120]{1,0:T(8,128)(2,1)S(1)} %fusion.50, bf16[48,5120]{1,0:T(8,128)(2,1)S(1)} %collective-permute-done, f32[]{:T(128)} %bitcast.13, f32[]{:T(128)} %bitcast.12, f32[]{:T(128)} %bitcast), kind=kLoop, calls=%fused_computation.46 | loop fusion | flops 2457600 | bytes 1966092 | tf_op jit(solution)/shard_map/broadcast_in_dim | solution.py:79
  (1 shorter events, 0.0 us)
Async XLA Ops:
  6.5 45.6 %copy-start = (bf16[1,128,5120]{2,1,0:T(8,128)(2,1)S(1)}, bf16[1,128,5120]{2,1,0:T(8,128)(2,1)}, u32[]{:S(2)}) copy-start(bf16[1,128,5120]{2,1,0:T(8,128)(2,1)} %param.7) | copy-start | bytes 3932164
  6.5 45.6 %all-gather.2.cloned.1.call-start = ((), (), s32[]{:S(2)}) async-start(), calls=%async_computation.1 | async-start | bytes 2457600 | tf_op jit(solution)/shard_map/all_gather | solution.py:30
  7.3 47.4 %copy-start.1 = (bf16[1,128,5120]{2,1,0:T(8,128)(2,1)S(1)}, bf16[1,128,5120]{2,1,0:T(8,128)(2,1)}, u32[]{:S(2)}) copy-start(bf16[1,128,5120]{2,1,0:T(8,128)(2,1)} %param.8) | copy-start | bytes 3932164
  7.3 100.7 %reduce-scatter.2.cloned.1.call-start = ((), (), s32[]{:S(2)}) async-start(), calls=%async_computation.2 | async-start | bytes 2457600 | tf_op jit(solution)/shard_map/reduce_scatter | solution.py:57
  57.6 3.4 %copy-start.2 = (bf16[1,128,5120]{2,1,0:T(8,128)(2,1)S(1)}, bf16[1,128,5120]{2,1,0:T(8,128)(2,1)}, u32[]{:S(2)}) copy-start(bf16[1,128,5120]{2,1,0:T(8,128)(2,1)} %param.9) | copy-start | bytes 3932164
  66.8 41.2 %copy-start.3 = (bf16[1,48,5120]{2,1,0:T(8,128)(2,1)S(1)}, bf16[1,48,5120]{2,1,0:T(8,128)(2,1)}, u32[]{:S(2)}) copy-start(bf16[1,48,5120]{2,1,0:T(8,128)(2,1)} %param.10) | copy-start | bytes 1474564
  66.8 41.2 %copy-start.4 = (bf16[1,48,5120]{2,1,0:T(8,128)(2,1)S(1)}, bf16[1,48,5120]{2,1,0:T(8,128)(2,1)}, u32[]{:S(2)}) copy-start(bf16[1,48,5120]{2,1,0:T(8,128)(2,1)} %param.12) | copy-start | bytes 1474564
  66.8 41.2 %copy-start.5 = (bf16[1,48,5120]{2,1,0:T(8,128)(2,1)S(1)}, bf16[1,48,5120]{2,1,0:T(8,128)(2,1)}, u32[]{:S(2)}) copy-start(bf16[1,48,5120]{2,1,0:T(8,128)(2,1)} %param.11) | copy-start | bytes 1474564
  66.8 44.9 %copy-start.6 = (s32[1,3]{1,0:T(1,128)S(1)}, s32[1,3]{1,0:T(1,128)}, u32[]{:S(2)}) copy-start(s32[1,3]{1,0:T(1,128)} %param.13) | copy-start | bytes 40
  109.9 12.0 %collective-permute-start = (bf16[48,5120]{1,0:T(8,128)(2,1)S(1)}, bf16[48,5120]{1,0:T(8,128)(2,1)S(1)}, u32[]{:S(2)}, u32[]{:S(2)}) collective-permute-start(bf16[48,5120]{1,0:T(8,128)(2,1)S(1)} %fusion.50), channel_id=1, source_target_pairs={{0,4},{4,8},{8,12},{12,16},{16,20},{20,24},{24,28},{28,0},{1,5},{5... | collective-permute-start | bytes 1474568 | tf_op jit(solution)/shard_map/ppermute | solution.py:17
  111.7 12.7 %collective-permute-start.1 = (bf16[48,5120]{1,0:T(8,128)(2,1)S(1)}, bf16[48,5120]{1,0:T(8,128)(2,1)S(1)}, u32[]{:S(2)}, u32[]{:S(2)}) collective-permute-start(bf16[48,5120]{1,0:T(8,128)(2,1)S(1)} %fusion.50), channel_id=1, source_target_pairs={{0,28},{4,0},{8,4},{12,8},{16,12},{20,16},{24,20},{28,24},{1,29},{... | collective-permute-start | bytes 1474568 | tf_op jit(solution)/shard_map/ppermute | solution.py:17
Sparse Core Ops, SparseCore 0:
  8.9 43.1 all-gather.1
  66.9 40.9 reduce-scatter.1
where the time goes:
time: 136 us; the launch traced here: 134 us
  waiting for transfers between devices  98.7 us (73%)
  between operations  13.4 us (10%)
  matrix products  11.9 us (9%)
  other arithmetic  7.59 us (6%)
  starting transfers between devices  1.86 us (1%)
    all_gather x1, waiting for transfers between devices, shards(): full_rows = lax.all_gather(adapters, 'fsdp', axis=1, tiled=True)[0]  44.8 us
    reduce_scatter x1, waiting for transfers between devices, shards(): lax.psum_scatter(owned_rows(jnp.int32(0), lax.axis_size('fsdp') * shard_r...  41.1 us
    ppermute x2, waiting for transfers between devices, shifted(): lax.ppermute(array, axis, [(i, (i + by) % length) for i in range(length)])  12 us
    dot_general x4, matrix products, contract_tokens(): lax.dot_general(left, right, (((0,), (0,)), ((), ())), preferred_element_...  11.9 us
    broadcast_in_dim x1, other arithmetic, shards(): return results[None]  2.89 us
    concatenate x1, other arithmetic, shards(): jnp.concatenate([contract_tokens(left, right, scale) for left, right, sca...  2.75 us
  transfers between devices with their start and end apart: 4, of which 4 were waited for; matrix products, arithmetic and copies ran while one was open for 0% of the time, Pallas kernels for 0%

commit v1 on v0

v1 whole, which is shorter than its diff:
```python
import functools
import math

import jax
import jax.numpy as jnp
from jax import lax
from jax.experimental import pallas as pl
from jax.experimental.pallas import tpu as pltpu
from jax.sharding import PartitionSpec as P

beta_one = 0.9
beta_two = 0.999
learn_rate = 0.2
decay_rate = 0.5
epsilon = 1e-08

MESH = pl.DeviceIdType.MESH
CHUNKS = 10
LAG_SUM = 2
LAG_MIX = 3


def shifted(array, axis, by):
    length = lax.axis_size(axis)
    return lax.ppermute(array, axis, [(i, (i + by) % length) for i in range(length)])


def contract_tokens(left, right, scale):
    return (
        lax.dot_general(left, right, (((0,), (0,)), ((), ())), preferred_element_type=jnp.float32)
        * scale
    )


def adamw(params, first, second, gradient):
    new_first = beta_one * first + (1.0 - beta_one) * gradient
    new_second = beta_two * second + (1.0 - beta_two) * gradient * gradient
    first_hat = new_first / (1.0 - beta_one**2)
    second_hat = new_second / (1.0 - beta_two**2)
    step = first_hat / (jnp.sqrt(second_hat) + epsilon) + decay_rate * params
    return (params - learn_rate * step).astype(jnp.bfloat16)


def shards(hidden, grad_query, grad_value, adapters, first_moment, second_moment, mixing):
    tokens = hidden[0]
    width = tokens.shape[1]
    full_rows = lax.all_gather(adapters, "fsdp", axis=1, tiled=True)[0]
    rank = full_rows.shape[0] // 4
    inv_width = 1.0 / math.sqrt(width)
    inv_rank = 1.0 / math.sqrt(rank)
    factors = []
    for index, cot in ((0, grad_query[0]), (1, grad_value[0])):
        down = full_rows[2 * index * rank : (2 * index + 1) * rank]
        up_rows = full_rows[(2 * index + 1) * rank : (2 * index + 2) * rank]
        lowrank = (jnp.dot(tokens, down.T, preferred_element_type=jnp.float32) * inv_width).astype(
            jnp.bfloat16
        )
        back = (jnp.dot(cot, up_rows.T, preferred_element_type=jnp.float32) * inv_rank).astype(
            jnp.bfloat16
        )
        factors.append((back, tokens, inv_width))
        factors.append((lowrank, cot, inv_rank))
    group_tokens = tokens.shape[0] * lax.axis_size("fsdp")
    weights = mixing[0].astype(jnp.float32)
    term = jnp.concatenate(
        [contract_tokens(left, right, scale) for left, right, scale in factors], axis=0
    )
    gradient = (
        lax.psum_scatter(
            term.astype(jnp.bfloat16), "fsdp", scatter_dimension=0, tiled=True
        ).astype(jnp.float32)
        / group_tokens
    )
    updated = adamw(
        adapters[0].astype(jnp.float32),
        first_moment[0].astype(jnp.float32),
        second_moment[0].astype(jnp.float32),
        gradient,
    )
    lower = shifted(updated, "blk", 1)
    upper = shifted(updated, "blk", -1)
    total = weights[0] * lower.astype(jnp.float32) + weights[1] * updated.astype(jnp.float32)
    total = total + weights[2] * upper.astype(jnp.float32)
    results = (total / 4.0).astype(jnp.bfloat16)
    return results[None]


def kernel(
    groups,
    x_hbm,
    gq_hbm,
    gv_hbm,
    ad_hbm,
    fm_hbm,
    sm_hbm,
    mix_ref,
    out_ref,
    mats,
    full,
    own,
    first,
    second,
    fac,
    stage,
    sums,
    upd,
    low,
    high,
    ld_sem,
    ag_send,
    ag_recv,
    rs_send,
    rs_recv,
    go_send,
    go_recv,
):
    z = lax.axis_index("fsdp")
    b = lax.axis_index("blk")
    rows, width = ad_hbm.shape
    tokens = x_hbm.shape[0]
    cols = width // CHUNKS
    inv_width = 1.0 / math.sqrt(width)
    inv_rank = 1.0 / math.sqrt(rows)
    group_tokens = tokens * 4
    half = z // 2
    inner = z + 1 - 2 * half
    outer = z - 1 + 2 * half
    is_end = (z == 0) | (z == 3)
    is_mid = (z == 1) | (z == 2)
    above = lax.rem(b + 1, groups)
    below = lax.rem(b + groups - 1, groups)

    def g(s):
        return s + half * (3 - 2 * s)

    def mat_of(s):
        return (s % 2) * (s // 2 + 1)

    def scale_of(s):
        return jnp.where(s % 2 == 0, jnp.float32(inv_width), jnp.float32(inv_rank))

    def span(c):
        return pl.ds(pl.multiple_of(c * cols, 128), cols)

    loads = [
        pltpu.make_async_copy(ad_hbm, own, ld_sem.at[0]),
        pltpu.make_async_copy(x_hbm, mats.at[0], ld_sem.at[1]),
        pltpu.make_async_copy(gq_hbm, mats.at[1], ld_sem.at[2]),
        pltpu.make_async_copy(gv_hbm, mats.at[2], ld_sem.at[3]),
        pltpu.make_async_copy(fm_hbm, first, ld_sem.at[4]),
        pltpu.make_async_copy(sm_hbm, second, ld_sem.at[5]),
    ]
    for load in loads:
        load.start()

    barrier = pltpu.get_barrier_semaphore()
    pl.semaphore_signal(barrier, inc=1, device_id={"fsdp": inner}, device_id_type=MESH)
    pl.semaphore_signal(barrier, inc=1, device_id={"blk": above}, device_id_type=MESH)
    pl.semaphore_signal(barrier, inc=1, device_id={"blk": below}, device_id_type=MESH)

    @pl.when(is_mid)
    def _():
        pl.semaphore_signal(barrier, inc=1, device_id={"fsdp": outer}, device_id_type=MESH)
        pl.semaphore_wait(barrier, 4)

    @pl.when(is_end)
    def _():
        pl.semaphore_wait(barrier, 3)

    def gather(s, src, c, slot, to):
        return pltpu.make_async_remote_copy(
            src_ref=src.at[:, span(c)],
            dst_ref=full.at[s, :, span(c)],
            send_sem=ag_send.at[slot, c],
            recv_sem=ag_recv.at[s, c],
            device_id={"fsdp": to},
            device_id_type=MESH,
        )

    def pass_sum(src_slot, dst_slot, c, to):
        return pltpu.make_async_remote_copy(
            src_ref=stage.at[src_slot, :, span(c)],
            dst_ref=sums.at[dst_slot, :, span(c)],
            send_sem=rs_send.at[src_slot, c],
            recv_sem=rs_recv.at[dst_slot, c],
            device_id={"fsdp": to},
            device_id_type=MESH,
        )

    def gossip(c, way):
        return pltpu.make_async_remote_copy(
            src_ref=upd.at[:, span(c)],
            dst_ref=(low if way == 0 else high).at[:, span(c)],
            send_sem=go_send.at[way, c],
            recv_sem=go_recv.at[way, c],
            device_id={"blk": above if way == 0 else below},
            device_id_type=MESH,
        )

    def wait_shard(s, c):
        gather(s, full.at[s], c, 0, inner).wait_recv()

    def wait_sum(slot, c):
        pass_sum(0, slot, c, inner).wait_recv()

    def each(body):
        def step(c, carry):
            body(c)
            return carry

        lax.fori_loop(0, CHUNKS, step, 0)

    def product(s, block, c):
        return lax.dot_general(
            block,
            mats[mat_of(s), :, span(c)],
            (((1,), (1,)), ((), ())),
            preferred_element_type=jnp.float32,
        )

    def keep(s, acc):
        fac[s + 1 - 2 * (s % 2)] = (acc * scale_of(s)).astype(jnp.bfloat16)

    zero = jnp.zeros((rows, tokens), jnp.float32)

    def own_factor(s):
        keep(s, lax.fori_loop(0, CHUNKS, lambda c, acc: acc + product(s, own[:, span(c)], c), zero))

    def partial(k, c):
        return (
            jnp.dot(fac[k], mats[mat_of(k), :, span(c)], preferred_element_type=jnp.float32)
            * scale_of(k)
        )

    def finish(c, total):
        at = span(c)
        upd[:, at] = adamw(
            own[:, at].astype(jnp.float32),
            first[:, at].astype(jnp.float32),
            second[:, at].astype(jnp.float32),
            total / group_tokens,
        )
        gossip(c, 0).start()
        gossip(c, 1).start()

    weights = [mix_ref[0, j].astype(jnp.float32) for j in range(3)]

    def mix(c):
        at = span(c)
        gossip(c, 0).wait_recv()
        gossip(c, 1).wait_recv()
        total = weights[0] * low[:, at].astype(jnp.float32) + weights[1] * upd[:, at].astype(
            jnp.float32
        )
        total = total + weights[2] * high[:, at].astype(jnp.float32)
        out_ref[:, at] = (total / 4.0).astype(jnp.bfloat16)

    @pl.when(is_end)
    def _end():
        each(lambda c: gather(g(0), ad_hbm, c, 0, inner).start())
        for load in loads:
            load.wait()
        own_factor(g(0))

        def send_partial(slot, k):
            def body(c):
                stage[slot, :, span(c)] = partial(k, c).astype(jnp.bfloat16)
                pass_sum(slot, slot, c, inner).start()

            each(body)

        def receive(s):
            def body(c, acc):
                wait_shard(s, c)
                return acc + product(s, full[s, :, span(c)], c)

            keep(s, lax.fori_loop(0, CHUNKS, body, zero))

        send_partial(0, g(1))
        receive(g(1))
        receive(g(2))
        send_partial(1, g(3))
        receive(g(3))
        send_partial(2, g(2))

        def last(t, carry):
            @pl.when(t < CHUNKS)
            def _():
                wait_sum(0, t)
                finish(t, sums[0, :, span(t)].astype(jnp.float32) + partial(g(0), t))

            @pl.when(t >= LAG_MIX)
            def _():
                mix(t - LAG_MIX)

            return carry

        lax.fori_loop(0, CHUNKS + LAG_MIX, last, 0)
        each(lambda c: gather(g(0), ad_hbm, c, 0, inner).wait_send())

    @pl.when(is_mid)
    def _mid():
        def send_own(c):
            gather(g(1), ad_hbm, c, 0, outer).start()
            gather(g(1), ad_hbm, c, 1, inner).start()

        each(send_own)
        for load in loads:
            load.wait()
        own_factor(g(1))

        def near(c, accs):
            wait_shard(g(0), c)
            gather(g(0), full.at[g(0)], c, 2, inner).start()
            wait_shard(g(2), c)
            gather(g(2), full.at[g(2)], c, 3, outer).start()
            return (
                accs[0] + product(g(0), full[g(0), :, span(c)], c),
                accs[1] + product(g(2), full[g(2), :, span(c)], c),
            )

        acc_zero, acc_two = lax.fori_loop(0, CHUNKS, near, (zero, zero))
        keep(g(0), acc_zero)
        keep(g(2), acc_two)

        def far(c, acc):
            wait_shard(g(3), c)
            gather(g(3), full.at[g(3)], c, 4, outer).start()
            return acc + product(g(3), full[g(3), :, span(c)], c)

        keep(g(3), lax.fori_loop(0, CHUNKS, far, zero))

        def last(t, carry):
            @pl.when(t < 2 * CHUNKS)
            def _():
                m, c = t // CHUNKS, t % CHUNKS
                wait_sum(1 + m, c)
                total = sums[1 + m, :, span(c)].astype(jnp.float32) + partial(g(3 - m), c)
                stage[m, :, span(c)] = total.astype(jnp.bfloat16)
                pass_sum(m, 3 + m, c, inner).start()

            @pl.when((t >= LAG_SUM) & (t < CHUNKS + LAG_SUM))
            def _():
                c = t - LAG_SUM
                wait_sum(3, c)
                total = sums[3, :, span(c)].astype(jnp.float32) + partial(g(0), c)
                stage[2, :, span(c)] = total.astype(jnp.bfloat16)
                pass_sum(2, 0, c, outer).start()

            @pl.when((t >= CHUNKS + LAG_SUM) & (t < 2 * CHUNKS + LAG_SUM))
            def _():
                c = t - CHUNKS - LAG_SUM
                wait_sum(0, c)
                wait_sum(4, c)
                total = sums[0, :, span(c)].astype(jnp.float32) + partial(g(1), c)
                finish(c, total + sums[4, :, span(c)].astype(jnp.float32))

            @pl.when(t >= CHUNKS + LAG_SUM + LAG_MIX)
            def _():
                mix(t - CHUNKS - LAG_SUM - LAG_MIX)

            return carry

        lax.fori_loop(0, 2 * CHUNKS + LAG_SUM + LAG_MIX, last, 0)

        def sent(c):
            for slot in range(5):
                gather(g(1), ad_hbm, c, slot, inner).wait_send()

        each(sent)

    def drained(c):
        for slot in range(3):
            pass_sum(slot, 0, c, inner).wait_send()
        gossip(c, 0).wait_send()
        gossip(c, 1).wait_send()

    each(drained)


def fused(hidden, grad_query, grad_value, adapters, first_moment, second_moment, mixing):
    _, tokens, width = hidden.shape
    rows = adapters.shape[1]
    groups = lax.axis_size("blk")
    bf16 = jnp.bfloat16
    anywhere = pl.BlockSpec(memory_space=pl.ANY)
    shard = pltpu.VMEM((rows, width), bf16)
    out = pl.pallas_call(
        functools.partial(kernel, groups),
        out_shape=jax.ShapeDtypeStruct((rows, width), bf16),
        in_specs=[anywhere] * 6 + [pl.BlockSpec(memory_space=pltpu.SMEM)],
        out_specs=pl.BlockSpec(memory_space=pltpu.VMEM),
        scratch_shapes=[
            pltpu.VMEM((3, tokens, width), bf16),
            pltpu.VMEM((4, rows, width), bf16),
            shard,
            shard,
            shard,
            pltpu.VMEM((4, rows, tokens), bf16),
            pltpu.VMEM((3, rows, width), bf16),
            pltpu.VMEM((5, rows, width), bf16),
            shard,
            shard,
            shard,
            pltpu.SemaphoreType.DMA((6,)),
            pltpu.SemaphoreType.DMA((5, CHUNKS)),
            pltpu.SemaphoreType.DMA((4, CHUNKS)),
            pltpu.SemaphoreType.DMA((3, CHUNKS)),
            pltpu.SemaphoreType.DMA((5, CHUNKS)),
            pltpu.SemaphoreType.DMA((2, CHUNKS)),
            pltpu.SemaphoreType.DMA((2, CHUNKS)),
        ],
        compiler_params=pltpu.CompilerParams(collective_id=0, has_side_effects=True),
    )(
        hidden[0],
        grad_query[0],
        grad_value[0],
        adapters[0],
        first_moment[0],
        second_moment[0],
        mixing,
    )
    return out[None]


def solution(mesh):
    spec = P("blk", "fsdp", None)
    in_specs = (spec,) * 6 + (P("blk", None),)
    body = fused if mesh.shape["fsdp"] == 4 and mesh.shape["blk"] > 2 else shards
    return jax.shard_map(body, mesh=mesh, in_specs=in_specs, out_specs=spec, check_vma=False)
```

time: 136 us -> 66.4 us (0.49); the launches traced: 134 us -> 66.2 us
  waiting for transfers between devices: 98.7 us -> 0 us
  Pallas kernels: 0 us -> 64.4 us
  between operations: 13.4 us -> 0.01 us
  matrix products: 11.9 us -> 0 us
  other arithmetic: 7.59 us -> 0 us
  starting transfers between devices: 1.86 us -> 0 us
    pallas_call x0 -> x1, Pallas kernels: none -> 64.4 us  [fused(): pl.pallas_call(functools.partial(kernel, groups), out_shape=jax.ShapeDtyp...]
    all_gather x1 -> x0, waiting for transfers between devices: 44.8 us -> none  [shards(): full_rows = lax.all_gather(adapters, 'fsdp', axis=1, tiled=True)[0]]
    reduce_scatter x1 -> x0, waiting for transfers between devices: 41.1 us -> none  [shards(): lax.psum_scatter(owned_rows(jnp.int32(0), lax.axis_size('fsdp') * shard_r...]
    ppermute x2 -> x0, waiting for transfers between devices: 12 us -> none  [shifted(): lax.ppermute(array, axis, [(i, (i + by) % length) for i in range(length)])]
    dot_general x4 -> x0, matrix products: 11.9 us -> none  [contract_tokens(): lax.dot_general(left, right, (((0,), (0,)), ((), ())), preferred_element_...]
    broadcast_in_dim x1 -> x0, other arithmetic: 2.89 us -> none  [shards(): return results[None]]
    concatenate x1 -> x0, other arithmetic: 2.75 us -> none  [shards(): jnp.concatenate([contract_tokens(left, right, scale) for left, right, sca...]
    convert_element_type x2 -> x0, other arithmetic: 1.94 us -> none  [the longest x1 1.94 us: shards(): updated = (params - learn_rate * step).astype(jnp.bfloat16)]
  transfers between devices with their start and end apart: 4 -> 0, of which waited for: 4 -> 0; matrix products, arithmetic and copies ran while one was open for 0% -> 0% of each run, Pallas kernels for 0% -> 0%
where the time goes in v1:
time: 66.4 us; the launch traced here: 66.2 us
  Pallas kernels  64.4 us (97%)
  local copies, waits for them, and re-layouts  1.84 us (3%)
    pallas_call x1, Pallas kernels, fused(): pl.pallas_call(functools.partial(kernel, groups), out_shape=jax.ShapeDtyp...  64.4 us
    unnamed x1, local copies, waits for them, and re-layouts  1.84 us

profile of v1, /device:TPU:11, one launch (start us, length us, event | category | flops | bytes accessed | tf_op | source)
XLA Modules:
  0.0 66.2 jit_solution(10564719408689731073)
XLA Ops:
  0.0 64.4 %shard_map.73 = bf16[48,5120]{1,0:T(8,128)(2,1)} custom-call(bf16[128,5120]{1,0:T(8,128)(2,1)} %bitcast.8, bf16[128,5120]{1,0:T(8,128)(2,1)} %bitcast.9, bf16[128,5120]{1,0:T(8,128)(2,1)} %bitcast.10, bf16[48,5120]{1,0:T(8,128)(2,1)} %bitcast.11, bf16[48,5120]{1,0:T(8,128)(2,1)} %bitcast.12, bf16[48,5120]{1,0:T(8,128)(2,1)} %bitcast.13, s32[1,3]{1,0:T(1,128)} %mix_ref.1), custom_call_target="tpu_custom_call" | custom-call | tf_op jit(solution)/shard_map/pallas_call | solution.py:388
  64.4 1.8 %copy.9 = bf16[1,48,5120]{2,1,0:T(8,128)(2,1)} copy(bf16[1,48,5120]{2,1,0:T(8,128)(2,1)} %bitcast.7) | data formatting | bytes 983040

commit v2 on v1

--- a/solution.py
+++ b/solution.py
@@ -15,9 +15,13 @@
 epsilon = 1e-08
 
 MESH = pl.DeviceIdType.MESH
-CHUNKS = 10
-LAG_SUM = 2
-LAG_MIX = 3
+PARTS = 3
+STRIPS = 4
+CHUNKS = PARTS * STRIPS
+HEAD = 2 * STRIPS
+AHEAD = 3
+LAG_SUM = 4
+LAG_MIX = 5
 
 
 def shifted(array, axis, by):
@@ -101,6 +105,7 @@
     first,
     second,
     fac,
+    acc,
     stage,
     sums,
     upd,
@@ -118,7 +123,8 @@
     b = lax.axis_index("blk")
     rows, width = ad_hbm.shape
     tokens = x_hbm.shape[0]
-    cols = width // CHUNKS
+    cols = width // STRIPS
+    part_rows = rows // PARTS
     inv_width = 1.0 / math.sqrt(width)
     inv_rank = 1.0 / math.sqrt(rows)
     group_tokens = tokens * 4
@@ -140,7 +146,10 @@
         return jnp.where(s % 2 == 0, jnp.float32(inv_width), jnp.float32(inv_rank))
 
     def span(c):
-        return pl.ds(pl.multiple_of(c * cols, 128), cols)
+        return pl.ds(pl.multiple_of((c % STRIPS) * cols, 128), cols)
+
+    def block(c):
+        return pl.ds(pl.multiple_of((c // STRIPS) * part_rows, part_rows), part_rows), span(c)
 
     loads = [
         pltpu.make_async_copy(ad_hbm, own, ld_sem.at[0]),
@@ -169,8 +178,8 @@
 
     def gather(s, src, c, slot, to):
         return pltpu.make_async_remote_copy(
-            src_ref=src.at[:, span(c)],
-            dst_ref=full.at[s, :, span(c)],
+            src_ref=src,
+            dst_ref=full.at[s, c],
             send_sem=ag_send.at[slot, c],
             recv_sem=ag_recv.at[s, c],
             device_id={"fsdp": to},
@@ -179,8 +188,8 @@
 
     def pass_sum(src_slot, dst_slot, c, to):
         return pltpu.make_async_remote_copy(
-            src_ref=stage.at[src_slot, :, span(c)],
-            dst_ref=sums.at[dst_slot, :, span(c)],
+            src_ref=stage.at[src_slot, c],
+            dst_ref=sums.at[dst_slot, c],
             send_sem=rs_send.at[src_slot, c],
             recv_sem=rs_recv.at[dst_slot, c],
             device_id={"fsdp": to},
@@ -189,8 +198,8 @@
 
     def gossip(c, way):
         return pltpu.make_async_remote_copy(
-            src_ref=upd.at[:, span(c)],
-            dst_ref=(low if way == 0 else high).at[:, span(c)],
+            src_ref=upd.at[c],
+            dst_ref=(low if way == 0 else high).at[c],
             send_sem=go_send.at[way, c],
             recv_sem=go_recv.at[way, c],
             device_id={"blk": above if way == 0 else below},
@@ -198,46 +207,69 @@
         )
 
     def wait_shard(s, c):
-        gather(s, full.at[s], c, 0, inner).wait_recv()
+        gather(s, full.at[s, c], c, 0, inner).wait_recv()
 
     def wait_sum(slot, c):
         pass_sum(0, slot, c, inner).wait_recv()
 
-    def each(body):
+    def each(body, begin=0, end=CHUNKS):
         def step(c, carry):
             body(c)
             return carry
 
-        lax.fori_loop(0, CHUNKS, step, 0)
-
-    def product(s, block, c):
+        lax.fori_loop(begin, end, step, 0)
+
+    def product(s, left, c):
         return lax.dot_general(
-            block,
+            left,
             mats[mat_of(s), :, span(c)],
             (((1,), (1,)), ((), ())),
             preferred_element_type=jnp.float32,
         )
 
-    def keep(s, acc):
-        fac[s + 1 - 2 * (s % 2)] = (acc * scale_of(s)).astype(jnp.bfloat16)
-
-    zero = jnp.zeros((rows, tokens), jnp.float32)
+    def partner(s):
+        return s + 1 - 2 * (s % 2)
+
+    def absorb(s, slot, c):
+        term = product(s, full[s, c], c)
+
+        @pl.when(c % STRIPS == 0)
+        def _():
+            acc[slot] = term
+
+        @pl.when(c % STRIPS > 0)
+        def _():
+            acc[slot] += term
+
+        @pl.when(c % STRIPS == STRIPS - 1)
+        def _():
+            fac[partner(s), c // STRIPS] = (acc[slot] * scale_of(s)).astype(jnp.bfloat16)
 
     def own_factor(s):
-        keep(s, lax.fori_loop(0, CHUNKS, lambda c, acc: acc + product(s, own[:, span(c)], c), zero))
+        zero = jnp.zeros((rows, tokens), jnp.float32)
+        whole = lax.fori_loop(
+            0, STRIPS, lambda c, total: total + product(s, own[:, span(c)], c), zero
+        )
+        whole = (whole * scale_of(s)).astype(jnp.bfloat16)
+        for p in range(PARTS):
+            fac[partner(s), p] = whole[p * part_rows : (p + 1) * part_rows]
 
     def partial(k, c):
         return (
-            jnp.dot(fac[k], mats[mat_of(k), :, span(c)], preferred_element_type=jnp.float32)
+            jnp.dot(
+                fac[k, c // STRIPS],
+                mats[mat_of(k), :, span(c)],
+                preferred_element_type=jnp.float32,
+            )
             * scale_of(k)
         )
 
     def finish(c, total):
-        at = span(c)
-        upd[:, at] = adamw(
-            own[:, at].astype(jnp.float32),
-            first[:, at].astype(jnp.float32),
-            second[:, at].astype(jnp.float32),
+        at = block(c)
+        upd[c] = adamw(
+            own[at].astype(jnp.float32),
+            first[at].astype(jnp.float32),
+            second[at].astype(jnp.float32),
             total / group_tokens,
         )
         gossip(c, 0).start()
@@ -246,48 +278,50 @@
     weights = [mix_ref[0, j].astype(jnp.float32) for j in range(3)]
 
     def mix(c):
-        at = span(c)
+        at = block(c)
         gossip(c, 0).wait_recv()
         gossip(c, 1).wait_recv()
-        total = weights[0] * low[:, at].astype(jnp.float32) + weights[1] * upd[:, at].astype(
+        total = weights[0] * low[c].astype(jnp.float32) + weights[1] * upd[c].astype(
             jnp.float32
         )
-        total = total + weights[2] * high[:, at].astype(jnp.float32)
-        out_ref[:, at] = (total / 4.0).astype(jnp.bfloat16)
+        total = total + weights[2] * high[c].astype(jnp.float32)
+        out_ref[at] = (total / 4.0).astype(jnp.bfloat16)
 
     @pl.when(is_end)
     def _end():
-        each(lambda c: gather(g(0), ad_hbm, c, 0, inner).start())
+        each(lambda c: gather(g(0), ad_hbm.at[block(c)], c, 0, inner).start())
         for load in loads:
             load.wait()
         own_factor(g(0))
 
-        def send_partial(slot, k):
+        def send_partial(slot, k, c):
+            stage[slot, c] = partial(k, c).astype(jnp.bfloat16)
+            pass_sum(slot, slot, c, inner).start()
+
+        def receive(s, slot=None, k=None):
             def body(c):
-                stage[slot, :, span(c)] = partial(k, c).astype(jnp.bfloat16)
-                pass_sum(slot, slot, c, inner).start()
+                wait_shard(s, c)
+                absorb(s, 0, c)
+                if slot is not None:
+
+                    @pl.when(c % STRIPS == STRIPS - 1)
+                    def _():
+                        for j in range(STRIPS):
+                            send_partial(slot, k, c - (STRIPS - 1) + j)
 
             each(body)
 
-        def receive(s):
-            def body(c, acc):
-                wait_shard(s, c)
-                return acc + product(s, full[s, :, span(c)], c)
-
-            keep(s, lax.fori_loop(0, CHUNKS, body, zero))
-
-        send_partial(0, g(1))
+        each(lambda c: send_partial(0, g(1), c), 0, HEAD)
         receive(g(1))
-        receive(g(2))
-        send_partial(1, g(3))
-        receive(g(3))
-        send_partial(2, g(2))
+        receive(g(2), 1, g(3))
+        receive(g(3), 2, g(2))
+        each(lambda c: send_partial(0, g(1), c), HEAD, CHUNKS)
 
         def last(t, carry):
             @pl.when(t < CHUNKS)
             def _():
                 wait_sum(0, t)
-                finish(t, sums[0, :, span(t)].astype(jnp.float32) + partial(g(0), t))
+                finish(t, sums[0, t].astype(jnp.float32) + partial(g(0), t))
 
             @pl.when(t >= LAG_MIX)
             def _():
@@ -296,55 +330,55 @@
             return carry
 
         lax.fori_loop(0, CHUNKS + LAG_MIX, last, 0)
-        each(lambda c: gather(g(0), ad_hbm, c, 0, inner).wait_send())
+        each(lambda c: gather(g(0), ad_hbm.at[block(c)], c, 0, inner).wait_send())
 
     @pl.when(is_mid)
     def _mid():
         def send_own(c):
-            gather(g(1), ad_hbm, c, 0, outer).start()
-            gather(g(1), ad_hbm, c, 1, inner).start()
+            gather(g(1), ad_hbm.at[block(c)], c, 0, outer).start()
+            gather(g(1), ad_hbm.at[block(c)], c, 1, inner).start()
 
         each(send_own)
         for load in loads:
             load.wait()
         own_factor(g(1))
 
-        def near(c, accs):
+        def near(c):
             wait_shard(g(0), c)
-            gather(g(0), full.at[g(0)], c, 2, inner).start()
+            gather(g(0), full.at[g(0), c], c, 2, inner).start()
             wait_shard(g(2), c)
-            gather(g(2), full.at[g(2)], c, 3, outer).start()
-            return (
-                accs[0] + product(g(0), full[g(0), :, span(c)], c),
-                accs[1] + product(g(2), full[g(2), :, span(c)], c),
-            )
-
-        acc_zero, acc_two = lax.fori_loop(0, CHUNKS, near, (zero, zero))
-        keep(g(0), acc_zero)
-        keep(g(2), acc_two)
-
-        def far(c, acc):
+            gather(g(2), full.at[g(2), c], c, 3, outer).start()
+            absorb(g(0), 0, c)
+            absorb(g(2), 1, c)
+
+        each(near)
+
+        def far(c):
             wait_shard(g(3), c)
-            gather(g(3), full.at[g(3)], c, 4, outer).start()
-            return acc + product(g(3), full[g(3), :, span(c)], c)
-
-        keep(g(3), lax.fori_loop(0, CHUNKS, far, zero))
+            gather(g(3), full.at[g(3), c], c, 4, outer).start()
+            absorb(g(3), 0, c)
+
+        each(far, 0, CHUNKS - AHEAD)
 
         def last(t, carry):
+            @pl.when(t < AHEAD)
+            def _():
+                far(t + CHUNKS - AHEAD)
+
             @pl.when(t < 2 * CHUNKS)
             def _():
                 m, c = t // CHUNKS, t % CHUNKS
                 wait_sum(1 + m, c)
-                total = sums[1 + m, :, span(c)].astype(jnp.float32) + partial(g(3 - m), c)
-                stage[m, :, span(c)] = total.astype(jnp.bfloat16)
+                total = sums[1 + m, c].astype(jnp.float32) + partial(g(3 - m), c)
+                stage[m, c] = total.astype(jnp.bfloat16)
                 pass_sum(m, 3 + m, c, inner).start()
 
             @pl.when((t >= LAG_SUM) & (t < CHUNKS + LAG_SUM))
             def _():
                 c = t - LAG_SUM
                 wait_sum(3, c)
-                total = sums[3, :, span(c)].astype(jnp.float32) + partial(g(0), c)
-                stage[2, :, span(c)] = total.astype(jnp.bfloat16)
+                total = sums[3, c].astype(jnp.float32) + partial(g(0), c)
+                stage[2, c] = total.astype(jnp.bfloat16)
                 pass_sum(2, 0, c, outer).start()
 
             @pl.when((t >= CHUNKS + LAG_SUM) & (t < 2 * CHUNKS + LAG_SUM))
@@ -352,8 +386,8 @@
                 c = t - CHUNKS - LAG_SUM
                 wait_sum(0, c)
                 wait_sum(4, c)
-                total = sums[0, :, span(c)].astype(jnp.float32) + partial(g(1), c)
-                finish(c, total + sums[4, :, span(c)].astype(jnp.float32))
+                total = sums[0, c].astype(jnp.float32) + partial(g(1), c)
+                finish(c, total + sums[4, c].astype(jnp.float32))
 
             @pl.when(t >= CHUNKS + LAG_SUM + LAG_MIX)
             def _():
@@ -365,7 +399,7 @@
 
         def sent(c):
             for slot in range(5):
-                gather(g(1), ad_hbm, c, slot, inner).wait_send()
+                gather(g(1), ad_hbm.at[block(c)], c, slot, inner).wait_send()
 
         each(sent)
 
@@ -385,6 +419,7 @@
     bf16 = jnp.bfloat16
     anywhere = pl.BlockSpec(memory_space=pl.ANY)
     shard = pltpu.VMEM((rows, width), bf16)
+    chunks = (CHUNKS, rows // PARTS, width // STRIPS)
     out = pl.pallas_call(
         functools.partial(kernel, groups),
         out_shape=jax.ShapeDtypeStruct((rows, width), bf16),
@@ -392,16 +427,17 @@
         out_specs=pl.BlockSpec(memory_space=pltpu.VMEM),
         scratch_shapes=[
             pltpu.VMEM((3, tokens, width), bf16),
-            pltpu.VMEM((4, rows, width), bf16),
+            pltpu.VMEM((4, *chunks), bf16),
             shard,
             shard,
             shard,
-            pltpu.VMEM((4, rows, tokens), bf16),
-            pltpu.VMEM((3, rows, width), bf16),
-            pltpu.VMEM((5, rows, width), bf16),
-            shard,
-            shard,
-            shard,
+            pltpu.VMEM((4, PARTS, rows // PARTS, tokens), bf16),
+            pltpu.VMEM((2, rows // PARTS, tokens), jnp.float32),
+            pltpu.VMEM((3, *chunks), bf16),
+            pltpu.VMEM((5, *chunks), bf16),
+            pltpu.VMEM(chunks, bf16),
+            pltpu.VMEM(chunks, bf16),
+            pltpu.VMEM(chunks, bf16),
             pltpu.SemaphoreType.DMA((6,)),
             pltpu.SemaphoreType.DMA((5, CHUNKS)),
             pltpu.SemaphoreType.DMA((4, CHUNKS)),

time: 66.4 us -> 57.3 us (0.86)
  Pallas kernels: 64.4 us -> 55 us
    pallas_call x1, Pallas kernels: 64.4 us -> 55 us  [fused(): pl.pallas_call(functools.partial(kernel, groups), out_shape=jax.ShapeDtyp...]
where the time goes in v2:
time: 57.3 us; the launch traced here: 56.9 us
  Pallas kernels  55 us (96%)
  local copies, waits for them, and re-layouts  1.84 us (3%)
    pallas_call x1, Pallas kernels, fused(): pl.pallas_call(functools.partial(kernel, groups), out_shape=jax.ShapeDtyp...  55 us
    unnamed x1, local copies, waits for them, and re-layouts  1.84 us

profile of v2, /device:TPU:11, one launch (start us, length us, event | category | flops | bytes accessed | tf_op | source)
XLA Modules:
  0.0 56.9 jit_solution(6294873673707913644)
XLA Ops:
  0.0 55.0 %shard_map.73 = bf16[48,5120]{1,0:T(8,128)(2,1)} custom-call(bf16[128,5120]{1,0:T(8,128)(2,1)} %bitcast.8, bf16[128,5120]{1,0:T(8,128)(2,1)} %bitcast.9, bf16[128,5120]{1,0:T(8,128)(2,1)} %bitcast.10, bf16[48,5120]{1,0:T(8,128)(2,1)} %bitcast.11, bf16[48,5120]{1,0:T(8,128)(2,1)} %bitcast.12, bf16[48,5120]{1,0:T(8,128)(2,1)} %bitcast.13, s32[1,3]{1,0:T(1,128)} %mix_ref.1), custom_call_target="tpu_custom_call" | custom-call | tf_op jit(solution)/shard_map/pallas_call | solution.py:423
  55.0 1.8 %copy.9 = bf16[1,48,5120]{2,1,0:T(8,128)(2,1)} copy(bf16[1,48,5120]{2,1,0:T(8,128)(2,1)} %bitcast.7) | data formatting | bytes 983040

commit v3 on v2

--- a/solution.py
+++ b/solution.py
@@ -16,12 +16,12 @@
 
 MESH = pl.DeviceIdType.MESH
 PARTS = 3
-STRIPS = 4
+STRIPS = 2
 CHUNKS = PARTS * STRIPS
 HEAD = 2 * STRIPS
-AHEAD = 3
-LAG_SUM = 4
-LAG_MIX = 5
+AHEAD = 2
+LAG_SUM = 2
+LAG_MIX = 3
 
 
 def shifted(array, axis, by):
@@ -289,8 +289,9 @@
 
     @pl.when(is_end)
     def _end():
-        each(lambda c: gather(g(0), ad_hbm.at[block(c)], c, 0, inner).start())
-        for load in loads:
+        loads[0].wait()
+        each(lambda c: gather(g(0), own.at[block(c)], c, 0, inner).start())
+        for load in loads[1:]:
             load.wait()
         own_factor(g(0))
 
@@ -330,16 +331,17 @@
             return carry
 
         lax.fori_loop(0, CHUNKS + LAG_MIX, last, 0)
-        each(lambda c: gather(g(0), ad_hbm.at[block(c)], c, 0, inner).wait_send())
+        each(lambda c: gather(g(0), own.at[block(c)], c, 0, inner).wait_send())
 
     @pl.when(is_mid)
     def _mid():
         def send_own(c):
-            gather(g(1), ad_hbm.at[block(c)], c, 0, outer).start()
-            gather(g(1), ad_hbm.at[block(c)], c, 1, inner).start()
-
+            gather(g(1), own.at[block(c)], c, 0, outer).start()
+            gather(g(1), own.at[block(c)], c, 1, inner).start()
+
+        loads[0].wait()
         each(send_own)
-        for load in loads:
+        for load in loads[1:]:
             load.wait()
         own_factor(g(1))
 
@@ -399,7 +401,7 @@
 
         def sent(c):
             for slot in range(5):
-                gather(g(1), ad_hbm.at[block(c)], c, slot, inner).wait_send()
+                gather(g(1), own.at[block(c)], c, slot, inner).wait_send()
 
         each(sent)
 
@@ -422,7 +424,7 @@
     chunks = (CHUNKS, rows // PARTS, width // STRIPS)
     out = pl.pallas_call(
         functools.partial(kernel, groups),
-        out_shape=jax.ShapeDtypeStruct((rows, width), bf16),
+        out_shape=pltpu.VMEM((rows, width), bf16),
         in_specs=[anywhere] * 6 + [pl.BlockSpec(memory_space=pltpu.SMEM)],
         out_specs=pl.BlockSpec(memory_space=pltpu.VMEM),
         scratch_shapes=[
@@ -446,7 +448,7 @@
             pltpu.SemaphoreType.DMA((2, CHUNKS)),
             pltpu.SemaphoreType.DMA((2, CHUNKS)),
         ],
-        compiler_params=pltpu.CompilerParams(collective_id=0, has_side_effects=True),
+        compiler_params=pltpu.CompilerParams(collective_id=0, has_side_effects=True, vmem_limit_bytes=66306048),
     )(
         hidden[0],
         grad_query[0],

time: 57.3 us -> 54.7 us (0.955)
  Pallas kernels: 55 us -> 53.3 us
  local copies, waits for them, and re-layouts: 1.84 us -> 0.78 us
    pallas_call x1, Pallas kernels: 55 us -> 53.3 us  [fused(): pl.pallas_call(functools.partial(kernel, groups), out_shape=pltpu.VMEM((r...]
    unnamed x1, local copies, waits for them, and re-layouts: 1.84 us -> 0.78 us
where the time goes in v3:
time: 54.7 us; the launch traced here: 54.1 us
  Pallas kernels  53.3 us (97%)
  local copies, waits for them, and re-layouts  0.78 us (1%)
    pallas_call x1, Pallas kernels, fused(): pl.pallas_call(functools.partial(kernel, groups), out_shape=pltpu.VMEM((r...  53.3 us

profile of v3, /device:TPU:11, one launch (start us, length us, event | category | flops | bytes accessed | tf_op | source)
XLA Modules:
  0.0 54.1 jit_solution(9399461070859007410)
XLA Ops:
  0.0 53.3 %shard_map.73 = bf16[48,5120]{1,0:T(8,128)(2,1)S(1)} custom-call(bf16[128,5120]{1,0:T(8,128)(2,1)} %bitcast.8, bf16[128,5120]{1,0:T(8,128)(2,1)} %bitcast.9, bf16[128,5120]{1,0:T(8,128)(2,1)} %bitcast.10, bf16[48,5120]{1,0:T(8,128)(2,1)} %bitcast.11, bf16[48,5120]{1,0:T(8,128)(2,1)} %bitcast.12, bf16[48,5120]{1,0:T(8,128)(2,1)} %bitcast.13, s32[1,3]{1,0:T(1,128)} %mix_ref.1), custom_call_target="tpu_custom_call" | custom-call | tf_op jit(solution)/shard_map/pallas_call | solution.py:425
  53.3 0.8 %copy.9 = bf16[1,48,5120]{2,1,0:T(8,128)(2,1)} copy(bf16[1,48,5120]{2,1,0:T(8,128)(2,1)S(1)} %bitcast.7) | data formatting | bytes 983040
